TPU v7x, 32 devices: a whole 2x2x4 slice. The times are simulated.
32 devices in a mesh: group: 2 (over y), clip: 4 (over z), pix: 4 (over x, core).
Axes of the slice: x: 2, y: 2, z: 4, core: 2. Of those that a mesh axis runs over, the one named last changes fastest.
Arguments:
- latents: bfloat16 [64, 256, 320], P(('group', 'clip'), 'pix'), parts along dimension 0, may hold values from -6 to 6
- sampled: int32 [8], P(('group', 'clip')), parts along dimension 0, may hold values from 0 to 7
- temporal_gain: float32 [320], replicated, may hold values from 0.5 to 1.5
- temporal_qkv: bfloat16 [320, 960], replicated, may hold values from -64 to 64
- temporal_out: bfloat16 [320, 320], replicated, may hold values from -0.3125 to 0.3125
- spatial_gain: float32 [320], replicated, may hold values from 0.5 to 1.5
- spatial_qkv: bfloat16 [320, 960], replicated, may hold values from -64 to 64
- spatial_out: bfloat16 [320, 320], replicated, may hold values from -0.3125 to 0.3125
Outputs:
- refined: bfloat16 [64, 256, 320], P(('group', 'clip', 'pix')), parts along dimension 0
There are 2 independent parts, one for each index of `group`. A program takes and returns all parts, laid end to end along the dimension named above; an argument that names none is the same for every part. Nothing has to cross between parts.
All inputs are finite; a program needn't handle non-finite values.
Results may differ from a plain program's by a relative error of at most 0.014.
The roundings to bfloat16 on the way count: a program that leaves them out, or rounds other values in their place, can miss the bound.
Values may be sent and summed in bfloat16 or wider, within the bound.
No kernel may reach another device: no remote copies, remote signals or barrier semaphores. Data moves between devices by JAX's collectives and lax.ppermute only.
A program may use at most 64 MiB of HBM per device.

v0:
```python
import math
import jax
import jax.numpy as jnp
from jax import lax
from jax.sharding import PartitionSpec as P

HEADS = 5
HEAD_DIM = 64
HALO = 4


def with_halo(block, sides, width):
    for axis, dim in sides:
        count = lax.axis_size(axis)
        forward = [(i, i + 1) for i in range(count - 1)]
        backward = [(target, source) for source, target in forward]
        low = lax.ppermute(
            lax.slice_in_dim(block, block.shape[dim] - width, None, axis=dim), axis, forward
        )
        high = lax.ppermute(lax.slice_in_dim(block, 0, width, axis=dim), axis, backward)
        block = jnp.concatenate([low, block, high], axis=dim)
    return block


def layer_norm(frame_rows, scales):
    values = frame_rows.astype(jnp.float32)
    average = jnp.mean(values, axis=-1, keepdims=True)
    centred = values - average
    spread = jnp.mean(centred * centred, axis=-1, keepdims=True)
    return (centred * lax.rsqrt(spread + 1e-05) * scales).astype(jnp.bfloat16)


def project(frame_rows, matrix):
    shape = frame_rows.shape
    flat = frame_rows.reshape(-1, shape[-1])
    result = jnp.dot(flat, matrix, preferred_element_type=jnp.float32).astype(jnp.bfloat16)
    return result.reshape(shape[:-1] + (matrix.shape[1],))


def temporal_attend(queries, key_pairs, usable):
    count, pixels, channels = queries.shape
    depth = key_pairs.shape[0]
    keys = key_pairs[..., :channels].reshape(depth, pixels, HEADS, HEAD_DIM)
    values = key_pairs[..., channels:].reshape(depth, pixels, HEADS, HEAD_DIM)
    query_heads = queries.reshape(count, pixels, HEADS, HEAD_DIM)
    scores = jnp.einsum(
        "fphd,kphd->phfk", query_heads, keys, preferred_element_type=jnp.float32
    ) / math.sqrt(HEAD_DIM)
    scores = jnp.where(usable[None, None, None, :], scores, -1e30)
    highest = jnp.max(scores, axis=-1, keepdims=True)
    expo = jnp.exp(scores - highest)
    weights = (expo / jnp.sum(expo, axis=-1, keepdims=True)).astype(jnp.bfloat16)
    mixed = jnp.einsum("phfk,kphd->fphd", weights, values, preferred_element_type=jnp.float32)
    return mixed.reshape(count, pixels, channels).astype(jnp.bfloat16)


def spatial_frame(frame_rows, scales, qkv_matrix, out_matrix):
    pixels, channels = frame_rows.shape
    normed = layer_norm(frame_rows, scales)
    packed = jnp.dot(normed, qkv_matrix, preferred_element_type=jnp.float32).astype(jnp.bfloat16)
    heads_view = packed.reshape(pixels, 3, HEADS, HEAD_DIM).transpose(1, 2, 0, 3)
    block_rows = 512 if pixels % 512 == 0 else pixels

    def one_head(triple):
        queries, keys, values = triple

        def query_block(query_rows):
            scores = jnp.dot(query_rows, keys.T, preferred_element_type=jnp.float32) / math.sqrt(
                HEAD_DIM
            )
            highest = jnp.max(scores, axis=-1, keepdims=True)
            expo = jnp.exp(scores - highest)
            weights = (expo / jnp.sum(expo, axis=-1, keepdims=True)).astype(jnp.bfloat16)
            return jnp.dot(weights, values, preferred_element_type=jnp.float32).astype(jnp.bfloat16)

        blocks = lax.map(query_block, queries.reshape(pixels // block_rows, block_rows, HEAD_DIM))
        return blocks.reshape(pixels, HEAD_DIM)

    mixed = lax.map(one_head, (heads_view[0], heads_view[1], heads_view[2]))
    mixed = mixed.transpose(1, 0, 2).reshape(pixels, channels)
    update = jnp.dot(mixed, out_matrix, preferred_element_type=jnp.float32)
    return (frame_rows.astype(jnp.float32) + update).astype(jnp.bfloat16)


def body(
    latents,
    sampled,
    temporal_gain,
    temporal_qkv,
    temporal_out,
    spatial_gain,
    spatial_qkv,
    spatial_out,
):
    frames_here, pixel_count, channels = latents.shape
    normed = layer_norm(latents, temporal_gain)
    queries = project(normed, temporal_qkv[:, :channels])
    pair_matrix = temporal_qkv[:, channels:]
    picked = lax.dynamic_slice_in_dim(normed, sampled[0], 1, 0)
    global_pairs = project(lax.all_gather(picked, "clip", axis=0, tiled=True), pair_matrix)
    border_rows = with_halo(normed, (("clip", 0),), HALO)
    border = project(border_rows, pair_matrix)
    clip_index = lax.axis_index("clip")
    clip_count = lax.axis_size("clip")
    positions = (
        clip_index * frames_here - HALO + jnp.arange(frames_here + 2 * HALO, dtype=jnp.int32)
    )
    inside = (positions >= 0) & (positions < clip_count * frames_here)
    usable = jnp.concatenate([inside, jnp.ones((global_pairs.shape[0],), jnp.bool_)])
    attended = temporal_attend(queries, jnp.concatenate([border, global_pairs], 0), usable)
    update = jnp.dot(
        attended.reshape(-1, channels), temporal_out, preferred_element_type=jnp.float32
    )
    temporal_rows = (latents.astype(jnp.float32).reshape(-1, channels) + update).astype(
        jnp.bfloat16
    )
    pix_count = lax.axis_size("pix")
    per_device = frames_here // pix_count
    grouped = temporal_rows.reshape(pix_count, per_device, pixel_count, channels)
    frame_block = lax.all_to_all(grouped, "pix", split_axis=0, concat_axis=2, tiled=True)[0]
    result = lax.map(
        lambda frame_rows: spatial_frame(frame_rows, spatial_gain, spatial_qkv, spatial_out),
        frame_block,
    )
    whole = result[None]
    return whole.reshape(whole.shape[1], whole.shape[2], channels)


def solution(mesh):
    placed = (P(("group", "clip"), "pix", None), P(("group", "clip")), P(), P(), P(), P(), P(), P())
    return jax.shard_map(
        body,
        mesh=mesh,
        in_specs=placed,
        out_specs=P(("group", "clip", "pix"), None, None),
        check_vma=False,
    )
```

profile of v0, /device:TPU:0, one launch (start us, length us, event | category | flops | bytes accessed | tf_op | source)
XLA Modules:
  0.0 77.4 jit_solution(4738823542584057212)
XLA Ops:
  0.0 1.2 %convert_reduce_fusion.1 = f32[8,64]{1,0:T(8,128)S(1)} fusion(bf16[8,64,320]{2,1,0:T(8,128)(2,1)} %param.12), kind=kLoop, calls=%fused_computation.59 | loop fusion | flops 327168 | bytes 329728 | tf_op jit(solution)/shard_map/reduce_sum | solution.py:27
  1.2 1.3 %multiply_reduce_fusion = f32[8,64]{1,0:T(8,128)S(1)} fusion(bf16[8,64,320]{2,1,0:T(8,128)(2,1)} %param.12, f32[8,64]{1,0:T(8,128)S(1)} %broadcast_multiply_fusion.1), kind=kLoop, calls=%fused_computation.57 | loop fusion | flops 654848 | bytes 331776 | tf_op jit(solution)/shard_map/reduce_sum | solution.py:29
  2.5 1.2 %multiply_convert_fusion = bf16[8,64,320]{2,1,0:T(8,128)(2,1)S(1)} fusion(bf16[8,64,320]{2,1,0:T(8,128)(2,1)} %param.12, f32[320]{0:T(512)} %param.14, f32[8,64]{1,0:T(8,128)S(1)} %add_rsqrt_fusion.1, f32[8,64]{1,0:T(8,128)S(1)} %broadcast_multiply_fusion.1), kind=kLoop, calls=%fused_computation.56 | loop fusion | flops 819200 | bytes 660736 | tf_op jit(solution)/shard_map/convert_element_type | solution.py:30
  3.7 0.8 %fusion.38 = (bf16[4,64,320]{2,1,0:T(8,128)(2,1)}, bf16[4,64,320]{2,1,0:T(8,128)(2,1)}) fusion(bf16[8,64,320]{2,1,0:T(8,128)(2,1)S(1)} %multiply_convert_fusion), kind=kLoop, calls=%fused_computation.68 | loop fusion | bytes 655360 | tf_op jit(solution)/shard_map/slice | solution.py:18
  4.5 5.0 %collective-permute-start = (bf16[4,64,320]{2,1,0:T(8,128)(2,1)}, bf16[4,64,320]{2,1,0:T(8,128)(2,1)S(1)}, u32[]{:S(2)}, u32[]{:S(2)}) collective-permute-start(bf16[4,64,320]{2,1,0:T(8,128)(2,1)} %get-tuple-element.121), channel_id=1, source_target_pairs={{0,4},{4,8},{8,12},{1,5},{5,9},{9,13},{2,6},{6,10},{10,14},{3,7},{... | collective-permute-start | bytes 491528 | tf_op jit(solution)/shard_map/ppermute | solution.py:17
  9.5 1.3 %collective-permute-start.1 = (bf16[4,64,320]{2,1,0:T(8,128)(2,1)}, bf16[4,64,320]{2,1,0:T(8,128)(2,1)}, u32[]{:S(2)}, u32[]{:S(2)}) collective-permute-start(bf16[4,64,320]{2,1,0:T(8,128)(2,1)} %get-tuple-element.122), channel_id=1, source_target_pairs={{4,0},{8,4},{12,8},{5,1},{9,5},{13,9},{6,2},{10,6},{14,10},{7,3},{... | collective-permute-start | bytes 491528 | tf_op jit(solution)/shard_map/ppermute | solution.py:20
  11.5 16.6 %all_gather.3 = bf16[4,64,320]{2,1,0:T(8,128)(2,1)S(1)} all-gather(bf16[1,64,320]{2,1,0:T(8,128)(2,1)S(1)} %constant_dynamic-slice_fusion), channel_id=1, replica_groups=mesh['group'=2,'clip'=4,'pix'=4] {'clip'}, dimensions={0}, use_global_device_ids=true | all-gather | bytes 204800 | tf_op jit(solution)/shard_map/all_gather | solution.py:100
  28.5 0.5 convolution_convert_fusion.5
  28.9 1.1 %copy.26 = bf16[4,64,640]{1,2,0:T(8,128)(2,1)} copy(bf16[4,64,640]{2,1,0:T(8,128)(2,1)S(1)} %bitcast.127) | data formatting | bytes 655360 | tf_op jit(solution)/shard_map/reshape | solution.py:37
  30.4 0.6 copy.27
  31.0 1.0 %copy.31 = f32[512,320]{0,1:T(8,128)} copy(bf16[512,320]{1,0:T(8,128)(2,1)S(1)} %bitcast.121) | data formatting | bytes 983040 | tf_op jit(solution)/shard_map/reshape | solution.py:114
  32.0 1.1 %pad_maximum_fusion.1 = bf16[16,64,320]{2,1,0:T(8,128)(2,1)S(1)} fusion(bf16[4,64,320]{2,1,0:T(8,128)(2,1)} %collective-permute-done.1, bf16[8,64,320]{2,1,0:T(8,128)(2,1)S(1)} %multiply_convert_fusion, bf16[4,64,320]{2,1,0:T(8,128)(2,1)S(1)} %collective-permute-done), kind=kLoop, calls=%fused_computation.55 | loop fusion | flops 655360 | bytes 1310720 | tf_op jit(solution)/shard_map/concatenate | solution.py:21
  33.1 2.0 %convolution_convert_fusion.2 = bf16[1024,640]{1,0:T(8,128)(2,1)} fusion(bf16[1024,320]{1,0:T(8,128)(2,1)S(1)} %bitcast.124, bf16[320,960]{1,0:T(8,128)(2,1)S(1)} %copy-done.5), kind=kOutput, calls=%fused_computation.43 | convolution fusion | flops 420085760 | bytes 2506752 | tf_op jit(solution)/shard_map/dot_general | solution.py:36
  35.1 3.2 %copy.25 = bf16[16,64,640]{1,2,0:T(8,128)(2,1)S(1)} copy(bf16[16,64,640]{2,1,0:T(8,128)(2,1)} %bitcast.122) | data formatting | bytes 2621440 | tf_op jit(solution)/shard_map/reshape | solution.py:37
  38.4 3.6 %pad_maximum_fusion = (bf16[20,64,320]{1,2,0:T(8,128)(2,1)}, bf16[20,64,320]{1,2,0:T(8,128)(2,1)}) fusion(bf16[4,64,640]{1,2,0:T(8,128)(2,1)} %copy.26, bf16[16,64,640]{1,2,0:T(8,128)(2,1)S(1)} %copy.25), kind=kLoop, calls=%fused_computation.42 | loop fusion | flops 3276800 | bytes 3276800 | tf_op jit(solution)/shard_map/concatenate | solution.py:110
  42.0 2.9 %copy.28 = bf16[20,64,5,64]{3,0,2,1:T(8,128)(2,1)S(1)} copy(bf16[20,64,5,64]{1,3,2,0:T(8,128)(2,1)} %bitcast.120) | data formatting | bytes 1638400 | tf_op jit(solution)/shard_map/reshape | solution.py:43
  45.0 3.9 %copy.29 = bf16[20,64,5,64]{3,0,2,1:T(8,128)(2,1)} copy(bf16[20,64,5,64]{1,3,2,0:T(8,128)(2,1)} %bitcast.119) | data formatting | bytes 1638400 | tf_op jit(solution)/shard_map/reshape | solution.py:44
  48.8 2.3 %fusion.39 = (f32[64,5,8]{2,1,0:T(8,128)S(1)}, f32[64,5,8,20]{3,2,1,0:T(8,128)}) fusion(bf16[8,64,5,64]{3,0,2,1:T(8,128)(2,1)S(1)} %copy.27, bf16[20,64,5,64]{3,0,2,1:T(8,128)(2,1)S(1)} %copy.28, pred[20]{0:T(512)(128)(4,1)S(1)} %concatenate.11), kind=kOutput, calls=%fused_computation.69 | convolution fusion | flops 6758419 | bytes 1361940 | tf_op jit(solution)/shard_map/sub | solution.py:51
  51.1 2.7 %fusion.31 = bf16[8,64,5,64]{3,0,2,1:T(8,128)(2,1)S(1)} fusion(bf16[20,64,5,64]{3,0,2,1:T(8,128)(2,1)} %copy.29, f32[64,5,8,20]{3,2,1,0:T(8,128)} %get-tuple-element.124, f32[64,5,8]{2,1,0:T(8,128)S(1)} %get-tuple-element.123), kind=kOutput, calls=%fused_computation.50 | convolution fusion | flops 6819840 | bytes 1361920 | tf_op jit(solution)/shard_map/phfk,kphd->fphd/dot_general | solution.py:53
  53.8 0.6 copy.30
  55.3 0.9 %copy.32 = bf16[512,320]{1,0:T(8,128)(2,1)} copy(bf16[512,320]{0,1:T(8,128)(2,1)S(1)} %fusion.32) | data formatting | bytes 655360 | tf_op jit(solution)/shard_map/convert_element_type | solution.py:114
  56.2 3.5 %all-to-all-start = ((bf16[4,2,64,320]{3,2,1,0:T(8,128)(2,1)}), bf16[4,2,64,320]{3,2,1,0:T(8,128)(2,1)S(1)}, u32[]{:S(2)}, u32[]{:S(2)}) async-start(bf16[4,2,64,320]{3,2,1,0:T(8,128)(2,1)} %bitcast.23), calls=%async_computation | async-start | bytes 786432 | tf_op jit(solution)/shard_map/all_to_all | solution.py:120
  59.7 7.4 %all-to-all-done = bf16[4,2,64,320]{3,2,1,0:T(8,128)(2,1)S(1)} async-done(((bf16[4,2,64,320]{3,2,1,0:T(8,128)(2,1)}), bf16[4,2,64,320]{3,2,1,0:T(8,128)(2,1)S(1)}, u32[]{:S(2)}, u32[]{:S(2)}) %all-to-all-start) | async-done | bytes 327712 | tf_op jit(solution)/shard_map/all_to_all | solution.py:120
  67.3 10.0 %while.25 = (s32[]{:T(128)}, bf16[2,256,320]{1,2,0:T(8,128)(2,1)}, bf16[2,256,320]{1,2,0:T(8,128)(2,1)S(1)}, f32[320]{0:T(512)S(1)}, bf16[320,960]{1,0:T(8,128)(...) while((s32[]{:T(128)}, bf16[2,256,320]{1,2,0:T(8,128)(2,1)}, ...), condition=%wide.region_11.12_spmd, body=%wide.region_4.11_spmd.sunk | while | flops 228359936 | bytes 7997730 | solution.py:121
  67.5 0.5 convolution_convert_fusion.7
  68.1 0.5 copy.36
  68.7 2.6 %while.26 = (s32[]{:T(128)}, bf16[5,256,64]{1,2,0:T(8,128)(2,1)S(1)}, bf16[5,256,64]{2,1,0:T(8,128)(2,1)S(1)}, bf16[5,256,64]{2,1,0:T(8,128)(2,1)S(1)}, bf16[5,256,64]{2,1,0:T(8,128)(2,1)S(1)}, /*index=5*/s32[]{:T(128)}) while((s32[]{:T(128)}, bf16[5,256,64]{1,2,0:T(8,128)(2,1)S(1)}, bf16[5,256,64]{2,1,0:T(8,128)(2,1)S(1)}, ...), condition=%wide.region_10.10_spmd, body=%wide.region_7.9_spmd.sunk | while | flops 17251840 | bytes 1023045 | solution.py:79
  71.6 0.7 copy-done.8
  72.5 0.5 convolution_convert_fusion.7
  73.1 0.5 copy.36
  73.7 2.6 %while.26 = (s32[]{:T(128)}, bf16[5,256,64]{1,2,0:T(8,128)(2,1)S(1)}, bf16[5,256,64]{2,1,0:T(8,128)(2,1)S(1)}, bf16[5,256,64]{2,1,0:T(8,128)(2,1)S(1)}, bf16[5,256,64]{2,1,0:T(8,128)(2,1)S(1)}, /*index=5*/s32[]{:T(128)}) while((s32[]{:T(128)}, bf16[5,256,64]{1,2,0:T(8,128)(2,1)S(1)}, bf16[5,256,64]{2,1,0:T(8,128)(2,1)S(1)}, ...), condition=%wide.region_10.10_spmd, body=%wide.region_7.9_spmd.sunk | while | flops 17251840 | bytes 1023045 | solution.py:79
  76.6 0.7 copy-done.8
  (78 shorter events, 8.0 us)
Async XLA Ops:
  0.0 54.8 %copy-start = (bf16[320,320]{1,0:T(8,128)(2,1)S(1)}, bf16[320,320]{1,0:T(8,128)(2,1)}, u32[]{:S(2)}) copy-start(bf16[320,320]{1,0:T(8,128)(2,1)} %param.16) | copy-start | bytes 614404
  0.0 28.1 %copy-start.5 = (bf16[320,960]{1,0:T(8,128)(2,1)S(1)}, bf16[320,960]{1,0:T(8,128)(2,1)}, u32[]{:S(2)}) copy-start(bf16[320,960]{1,0:T(8,128)(2,1)} %param.15) | copy-start | bytes 1843204
  4.5 27.5 %collective-permute-start = (bf16[4,64,320]{2,1,0:T(8,128)(2,1)}, bf16[4,64,320]{2,1,0:T(8,128)(2,1)S(1)}, u32[]{:S(2)}, u32[]{:S(2)}) collective-permute-start(bf16[4,64,320]{2,1,0:T(8,128)(2,1)} %get-tuple-element.121), channel_id=1, source_target_pairs={{0,4},{4,8},{8,12},{1,5},{5,9},{9,13},{2,6},{6,10},{10,14},{3,7},{... | collective-permute-start | bytes 491528 | tf_op jit(solution)/shard_map/ppermute | solution.py:17
  9.5 22.5 %collective-permute-start.1 = (bf16[4,64,320]{2,1,0:T(8,128)(2,1)}, bf16[4,64,320]{2,1,0:T(8,128)(2,1)}, u32[]{:S(2)}, u32[]{:S(2)}) collective-permute-start(bf16[4,64,320]{2,1,0:T(8,128)(2,1)} %get-tuple-element.122), channel_id=1, source_target_pairs={{4,0},{8,4},{12,8},{5,1},{9,5},{13,9},{6,2},{10,6},{14,10},{7,3},{... | collective-permute-start | bytes 491528 | tf_op jit(solution)/shard_map/ppermute | solution.py:20
  28.9 2.0 %copy-start.2 = (bf16[8,64,320]{2,1,0:T(8,128)(2,1)S(1)}, bf16[8,64,320]{2,1,0:T(8,128)(2,1)}, u32[]{:S(2)}) copy-start(bf16[8,64,320]{2,1,0:T(8,128)(2,1)} %param.12) | copy-start | bytes 983044
  53.8 1.1 %copy-start.4 = (f32[512,320]{0,1:T(8,128)S(1)}, f32[512,320]{0,1:T(8,128)}, u32[]{:S(2)}) copy-start(f32[512,320]{0,1:T(8,128)} %copy.31) | copy-start | bytes 1966084
  55.3 12.0 %copy-start.1 = (bf16[320,960]{1,0:T(8,128)(2,1)S(1)}, bf16[320,960]{1,0:T(8,128)(2,1)}, u32[]{:S(2)}) copy-start(bf16[320,960]{1,0:T(8,128)(2,1)} %param.18) | copy-start | bytes 1843204
  55.3 12.0 %copy-start.3 = (bf16[320,320]{1,0:T(8,128)(2,1)S(1)}, bf16[320,320]{1,0:T(8,128)(2,1)}, u32[]{:S(2)}) copy-start(bf16[320,320]{1,0:T(8,128)(2,1)} %param.19) | copy-start | bytes 614404
  55.3 12.0 %copy-start.6 = (f32[320]{0:T(512)S(1)}, f32[320]{0:T(512)}, u32[]{:S(2)}) copy-start(f32[320]{0:T(512)} %param.17) | copy-start | bytes 3844
  56.2 10.8 %all-to-all-start = ((bf16[4,2,64,320]{3,2,1,0:T(8,128)(2,1)}), bf16[4,2,64,320]{3,2,1,0:T(8,128)(2,1)S(1)}, u32[]{:S(2)}, u32[]{:S(2)}) async-start(bf16[4,2,64,320]{3,2,1,0:T(8,128)(2,1)} %bitcast.23), calls=%async_computation | async-start | bytes 786432 | tf_op jit(solution)/shard_map/all_to_all | solution.py:120
  68.6 2.7 %copy-start.7 = (bf16[2,256,320]{1,2,0:T(8,128)(2,1)S(1)}, bf16[2,256,320]{1,2,0:T(8,128)(2,1)}, u32[]{:S(2)}) copy-start(bf16[2,256,320]{1,2,0:T(8,128)(2,1)} %get-tuple-element.244) | copy-start | bytes 983044 | tf_op jit(solution)/shard_map/while
  71.6 0.7 copy-start.8
  73.6 2.7 %copy-start.7 = (bf16[2,256,320]{1,2,0:T(8,128)(2,1)S(1)}, bf16[2,256,320]{1,2,0:T(8,128)(2,1)}, u32[]{:S(2)}) copy-start(bf16[2,256,320]{1,2,0:T(8,128)(2,1)} %get-tuple-element.244) | copy-start | bytes 983044 | tf_op jit(solution)/shard_map/while
  76.6 0.7 copy-start.8
where the time goes:
time: 77.9 us; the launch traced here: 77.4 us
  local copies, waits for them, and re-layouts  18.6 us (24%)
  blocking collectives  16.6 us (21%)
  matrix products  14.3 us (18%)
  starting transfers between devices  9.71 us (12%)
  other arithmetic  9.49 us (12%)
  waiting for transfers between devices  7.37 us (9%)
  between operations  0.92 us (1%)
    all_gather x1, blocking collectives, body(): lax.all_gather(picked, 'clip', axis=0, tiled=True)  16.6 us
    all_to_all x1, waiting for transfers between devices, body(): lax.all_to_all(grouped, 'pix', split_axis=0, concat_axis=2, tiled=True)[0]  7.37 us
    ppermute x1, starting transfers between devices, with_halo(): lax.ppermute(lax.slice_in_dim(block, block.shape[dim] - width, None, axis...  4.96 us
    reshape x2, local copies, waits for them, and re-layouts, project(): return result.reshape(shape[:-1] + (matrix.shape[1],))  4.31 us
    reshape x1, local copies, waits for them, and re-layouts, temporal_attend(): values = key_pairs[..., channels:].reshape(depth, pixels, HEADS, HEAD_DIM)  3.85 us
    concatenate x1, other arithmetic, body(): jnp.concatenate([border, global_pairs], 0)  3.64 us
    all_to_all x1, starting transfers between devices, body(): lax.all_to_all(grouped, 'pix', split_axis=0, concat_axis=2, tiled=True)[0]  3.46 us
    reshape x1, local copies, waits for them, and re-layouts, temporal_attend(): keys = key_pairs[..., :channels].reshape(depth, pixels, HEADS, HEAD_DIM)  2.93 us
  transfers between devices with their start and end apart: 3, of which 1 were waited for; matrix products, arithmetic and copies ran while one was open for 5% of the time, Pallas kernels for 0%

commit v1 on v0

--- a/solution.py
+++ b/solution.py
@@ -7,6 +7,29 @@
 HEADS = 5
 HEAD_DIM = 64
 HALO = 4
+
+
+def in_blocks(x, dim, size):
+    shape = x.shape
+    blocks = x.reshape(*shape[:dim], size, shape[dim] // size, *shape[dim + 1 :])
+    return jnp.moveaxis(blocks, dim, 0)
+
+
+def joined_along(parts, dim):
+    lengths = list(parts.shape[1:])
+    lengths[dim] *= parts.shape[0]
+    return jnp.moveaxis(parts, 0, dim).reshape(lengths)
+
+
+def sent_to_each(array, axis, split_dim, concat_dim):
+    size, position = (lax.axis_size(axis), lax.axis_index(axis))
+    tiles = in_blocks(array, split_dim, size)
+    outs = [tiles[position]]
+    for lap in range(1, size):
+        sent = tiles[(position + lap) % size]
+        outs.append(lax.ppermute(sent, axis, [(i, (i + lap) % size) for i in range(size)]))
+    tiles = jnp.stack(outs)[(position - jnp.arange(size)) % size]
+    return joined_along(tiles, concat_dim)
 
 
 def with_halo(block, sides, width):
@@ -117,7 +140,7 @@
     pix_count = lax.axis_size("pix")
     per_device = frames_here // pix_count
     grouped = temporal_rows.reshape(pix_count, per_device, pixel_count, channels)
-    frame_block = lax.all_to_all(grouped, "pix", split_axis=0, concat_axis=2, tiled=True)[0]
+    frame_block = sent_to_each(grouped, "pix", 0, 2)[0]
     result = lax.map(
         lambda frame_rows: spatial_frame(frame_rows, spatial_gain, spatial_qkv, spatial_out),
         frame_block,

time: 77.9 us -> 73.7 us (0.946)
  waiting for transfers between devices: 7.37 us -> 3.25 us
    all_to_all x1 -> x0, waiting for transfers between devices: 7.37 us -> none  [body(): lax.all_to_all(grouped, 'pix', split_axis=0, concat_axis=2, tiled=True)[0]]
    all_to_all x1 -> x0, starting transfers between devices: 3.46 us -> none  [body(): lax.all_to_all(grouped, 'pix', split_axis=0, concat_axis=2, tiled=True)[0]]
    ppermute x0 -> x3, waiting for transfers between devices: none -> 3.25 us  [sent_to_each(): lax.ppermute(sent, axis, [(i, (i + lap) % size) for i in range(size)])]
    ppermute x0 -> x3, starting transfers between devices: none -> 3 us  [sent_to_each(): lax.ppermute(sent, axis, [(i, (i + lap) % size) for i in range(size)])]
  transfers between devices with their start and end apart: 3 -> 5, of which waited for: 1 -> 3; matrix products, arithmetic and copies ran while one was open for 5% -> 5% of each run, Pallas kernels for 0% -> 0%
where the time goes in v1:
time: 73.7 us; the launch traced here: 72.9 us
  local copies, waits for them, and re-layouts  18.6 us (25%)
  blocking collectives  16.6 us (23%)
  matrix products  14.2 us (19%)
  other arithmetic  9.6 us (13%)
  starting transfers between devices  9.25 us (13%)
  waiting for transfers between devices  3.25 us (4%)
  between operations  1 us (1%)
    all_gather x1, blocking collectives, body(): lax.all_gather(picked, 'clip', axis=0, tiled=True)  16.6 us
    ppermute x1, starting transfers between devices, with_halo(): lax.ppermute(lax.slice_in_dim(block, block.shape[dim] - width, None, axis...  4.96 us
    reshape x2, local copies, waits for them, and re-layouts, project(): return result.reshape(shape[:-1] + (matrix.shape[1],))  4.31 us
    reshape x1, local copies, waits for them, and re-layouts, temporal_attend(): values = key_pairs[..., channels:].reshape(depth, pixels, HEADS, HEAD_DIM)  3.85 us
    concatenate x1, other arithmetic, body(): jnp.concatenate([border, global_pairs], 0)  3.64 us
    ppermute x3, waiting for transfers between devices, sent_to_each(): lax.ppermute(sent, axis, [(i, (i + lap) % size) for i in range(size)])  3.25 us
    ppermute x3, starting transfers between devices, sent_to_each(): lax.ppermute(sent, axis, [(i, (i + lap) % size) for i in range(size)])  3 us
    reshape x1, local copies, waits for them, and re-layouts, temporal_attend(): keys = key_pairs[..., :channels].reshape(depth, pixels, HEADS, HEAD_DIM)  2.93 us
  transfers between devices with their start and end apart: 5, of which 3 were waited for; matrix products, arithmetic and copies ran while one was open for 5% of the time, Pallas kernels for 0%

profile of v1, /device:TPU:0, one launch (start us, length us, event | category | flops | bytes accessed | tf_op | source)
XLA Modules:
  0.0 72.9 jit_solution(12725626316418151524)
XLA Ops:
  0.0 1.2 %convert_reduce_fusion.1 = f32[8,64]{1,0:T(8,128)S(1)} fusion(bf16[8,64,320]{2,1,0:T(8,128)(2,1)} %param.12), kind=kLoop, calls=%fused_computation.60 | loop fusion | flops 327168 | bytes 329728 | tf_op jit(solution)/shard_map/reduce_sum | solution.py:50
  1.2 1.3 %multiply_reduce_fusion = f32[8,64]{1,0:T(8,128)S(1)} fusion(bf16[8,64,320]{2,1,0:T(8,128)(2,1)} %param.12, f32[8,64]{1,0:T(8,128)S(1)} %broadcast_multiply_fusion.1), kind=kLoop, calls=%fused_computation.58 | loop fusion | flops 654848 | bytes 331776 | tf_op jit(solution)/shard_map/reduce_sum | solution.py:52
  2.5 1.2 %multiply_convert_fusion = bf16[8,64,320]{2,1,0:T(8,128)(2,1)S(1)} fusion(bf16[8,64,320]{2,1,0:T(8,128)(2,1)} %param.12, f32[320]{0:T(512)} %param.14, f32[8,64]{1,0:T(8,128)S(1)} %add_rsqrt_fusion.1, f32[8,64]{1,0:T(8,128)S(1)} %broadcast_multiply_fusion.1), kind=kLoop, calls=%fused_computation.57 | loop fusion | flops 819200 | bytes 660736 | tf_op jit(solution)/shard_map/convert_element_type | solution.py:53
  3.7 0.8 %fusion.40 = (bf16[4,64,320]{2,1,0:T(8,128)(2,1)}, bf16[4,64,320]{2,1,0:T(8,128)(2,1)}) fusion(bf16[8,64,320]{2,1,0:T(8,128)(2,1)S(1)} %multiply_convert_fusion), kind=kLoop, calls=%fused_computation.81 | loop fusion | bytes 655360 | tf_op jit(solution)/shard_map/slice | solution.py:41
  4.5 5.0 %collective-permute-start = (bf16[4,64,320]{2,1,0:T(8,128)(2,1)}, bf16[4,64,320]{2,1,0:T(8,128)(2,1)S(1)}, u32[]{:S(2)}, u32[]{:S(2)}) collective-permute-start(bf16[4,64,320]{2,1,0:T(8,128)(2,1)} %get-tuple-element.125), channel_id=1, source_target_pairs={{0,4},{4,8},{8,12},{1,5},{5,9},{9,13},{2,6},{6,10},{10,14},{3,7},{... | collective-permute-start | bytes 491528 | tf_op jit(solution)/shard_map/ppermute | solution.py:40
  9.5 1.3 %collective-permute-start.1 = (bf16[4,64,320]{2,1,0:T(8,128)(2,1)}, bf16[4,64,320]{2,1,0:T(8,128)(2,1)}, u32[]{:S(2)}, u32[]{:S(2)}) collective-permute-start(bf16[4,64,320]{2,1,0:T(8,128)(2,1)} %get-tuple-element.126), channel_id=1, source_target_pairs={{4,0},{8,4},{12,8},{5,1},{9,5},{13,9},{6,2},{10,6},{14,10},{7,3},{... | collective-permute-start | bytes 491528 | tf_op jit(solution)/shard_map/ppermute | solution.py:43
  11.5 16.6 %all_gather.3 = bf16[4,64,320]{2,1,0:T(8,128)(2,1)S(1)} all-gather(bf16[1,64,320]{2,1,0:T(8,128)(2,1)S(1)} %constant_dynamic-slice_fusion.1), channel_id=1, replica_groups=mesh['group'=2,'clip'=4,'pix'=4] {'clip'}, dimensions={0}, use_global_device_ids=true | all-gather | bytes 204800 | tf_op jit(solution)/shard_map/all_gather | solution.py:123
  29.0 1.1 %copy.26 = bf16[4,64,640]{1,2,0:T(8,128)(2,1)} copy(bf16[4,64,640]{2,1,0:T(8,128)(2,1)S(1)} %bitcast.141) | data formatting | bytes 655360 | tf_op jit(solution)/shard_map/reshape | solution.py:60
  30.4 0.6 copy.27
  31.0 1.0 %copy.31 = f32[512,320]{0,1:T(8,128)} copy(bf16[512,320]{1,0:T(8,128)(2,1)S(1)} %bitcast.134) | data formatting | bytes 983040 | tf_op jit(solution)/shard_map/reshape | solution.py:137
  32.1 1.1 %pad_maximum_fusion.1 = bf16[16,64,320]{2,1,0:T(8,128)(2,1)S(1)} fusion(bf16[4,64,320]{2,1,0:T(8,128)(2,1)} %collective-permute-done.1, bf16[8,64,320]{2,1,0:T(8,128)(2,1)S(1)} %multiply_convert_fusion, bf16[4,64,320]{2,1,0:T(8,128)(2,1)S(1)} %collective-permute-done), kind=kLoop, calls=%fused_computation.56 | loop fusion | flops 655360 | bytes 1310720 | tf_op jit(solution)/shard_map/concatenate | solution.py:44
  33.2 2.0 %convolution_convert_fusion.2 = bf16[1024,640]{1,0:T(8,128)(2,1)} fusion(bf16[1024,320]{1,0:T(8,128)(2,1)S(1)} %bitcast.137, bf16[320,960]{1,0:T(8,128)(2,1)S(1)} %copy-done.5), kind=kOutput, calls=%fused_computation.44 | convolution fusion | flops 420085760 | bytes 2506752 | tf_op jit(solution)/shard_map/dot_general | solution.py:59
  35.2 3.2 %copy.25 = bf16[16,64,640]{1,2,0:T(8,128)(2,1)S(1)} copy(bf16[16,64,640]{2,1,0:T(8,128)(2,1)} %bitcast.135) | data formatting | bytes 2621440 | tf_op jit(solution)/shard_map/reshape | solution.py:60
  38.4 3.6 %pad_maximum_fusion = (bf16[20,64,320]{1,2,0:T(8,128)(2,1)}, bf16[20,64,320]{1,2,0:T(8,128)(2,1)}) fusion(bf16[4,64,640]{1,2,0:T(8,128)(2,1)} %copy.26, bf16[16,64,640]{1,2,0:T(8,128)(2,1)S(1)} %copy.25), kind=kLoop, calls=%fused_computation.43 | loop fusion | flops 3276800 | bytes 3276800 | tf_op jit(solution)/shard_map/concatenate | solution.py:133
  42.1 2.9 %copy.28 = bf16[20,64,5,64]{3,0,2,1:T(8,128)(2,1)S(1)} copy(bf16[20,64,5,64]{1,3,2,0:T(8,128)(2,1)} %bitcast.133) | data formatting | bytes 1638400 | tf_op jit(solution)/shard_map/reshape | solution.py:66
  45.0 3.9 %copy.29 = bf16[20,64,5,64]{3,0,2,1:T(8,128)(2,1)} copy(bf16[20,64,5,64]{1,3,2,0:T(8,128)(2,1)} %bitcast.132) | data formatting | bytes 1638400 | tf_op jit(solution)/shard_map/reshape | solution.py:67
  48.9 2.3 %fusion.41 = (f32[64,5,8]{2,1,0:T(8,128)S(1)}, f32[64,5,8,20]{3,2,1,0:T(8,128)}) fusion(bf16[8,64,5,64]{3,0,2,1:T(8,128)(2,1)S(1)} %copy.27, bf16[20,64,5,64]{3,0,2,1:T(8,128)(2,1)S(1)} %copy.28, pred[20]{0:T(512)(128)(4,1)S(1)} %concatenate.11), kind=kOutput, calls=%fused_computation.82 | convolution fusion | flops 6758419 | bytes 1361940 | tf_op jit(solution)/shard_map/sub | solution.py:74
  51.2 2.7 %fusion.31 = bf16[8,64,5,64]{3,0,2,1:T(8,128)(2,1)S(1)} fusion(bf16[20,64,5,64]{3,0,2,1:T(8,128)(2,1)} %copy.29, f32[64,5,8,20]{3,2,1,0:T(8,128)} %get-tuple-element.128, f32[64,5,8]{2,1,0:T(8,128)S(1)} %get-tuple-element.127), kind=kOutput, calls=%fused_computation.51 | convolution fusion | flops 6819840 | bytes 1361920 | tf_op jit(solution)/shard_map/phfk,kphd->fphd/dot_general | solution.py:76
  53.9 0.6 copy.30
  55.7 1.6 %collective-permute-start.3 = (bf16[1,2,64,320]{3,2,1,0:T(8,128)(2,1)S(1)}, bf16[1,2,64,320]{3,2,1,0:T(8,128)(2,1)S(1)}, u32[]{:S(2)}, u32[]{:S(2)}) collective-permute-start(bf16[1,2,64,320]{3,2,1,0:T(8,128)(2,1)S(1)} %get-tuple-element.123), channel_id=1, source_target_pairs={{0,2},{1,3},{2,0},{3,1},{4,6},{5,7},{6,4},{7,5},{8,10},{9,11},{10,... | collective-permute-start | bytes 245768 | tf_op jit(solution)/shard_map/ppermute | solution.py:30
  57.3 1.4 %collective-permute-start.4 = (bf16[1,2,64,320]{3,2,1,0:T(8,128)(2,1)S(1)}, bf16[1,2,64,320]{3,2,1,0:T(8,128)(2,1)S(1)}, u32[]{:S(2)}, u32[]{:S(2)}) collective-permute-start(bf16[1,2,64,320]{3,2,1,0:T(8,128)(2,1)S(1)} %get-tuple-element.122), channel_id=1, source_target_pairs={{0,3},{1,0},{2,1},{3,2},{4,7},{5,4},{6,5},{7,6},{8,11},{9,8},{10,9... | collective-permute-start | bytes 245768 | tf_op jit(solution)/shard_map/ppermute | solution.py:30
  58.7 1.5 %collective-permute-done.2 = bf16[1,2,64,320]{3,2,1,0:T(8,128)(2,1)S(1)} collective-permute-done((bf16[1,2,64,320]{3,2,1,0:T(8,128)(2,1)S(1)}, bf16[1,2,64,320]{3,2,1,0:T(8,128)(2,1)S(1)}, u32[]{:S(2)}, u32[]{:S(2)}) %collective-permute-start.2) | collective-permute-done | bytes 81952 | tf_op jit(solution)/shard_map/ppermute | solution.py:30
  60.1 1.3 %collective-permute-done.3 = bf16[1,2,64,320]{3,2,1,0:T(8,128)(2,1)S(1)} collective-permute-done((bf16[1,2,64,320]{3,2,1,0:T(8,128)(2,1)S(1)}, bf16[1,2,64,320]{3,2,1,0:T(8,128)(2,1)S(1)}, u32[]{:S(2)}, u32[]{:S(2)}) %collective-permute-start.3) | collective-permute-done | bytes 81952 | tf_op jit(solution)/shard_map/ppermute | solution.py:30
  62.0 0.6 gather_fusion
  62.9 10.0 %while.25 = (s32[]{:T(128)}, bf16[2,256,320]{1,2,0:T(8,128)(2,1)}, bf16[2,256,320]{1,2,0:T(8,128)(2,1)S(1)}, f32[320]{0:T(512)S(1)}, bf16[320,960]{1,0:T(8,128)(...) while((s32[]{:T(128)}, bf16[2,256,320]{1,2,0:T(8,128)(2,1)}, ...), condition=%wide.region_11.12_spmd, body=%wide.region_4.11_spmd.sunk | while | flops 228359936 | bytes 7997730 | solution.py:144
  63.1 0.5 convolution_convert_fusion.7
  63.7 0.5 copy.36
  64.2 2.6 %while.26 = (s32[]{:T(128)}, bf16[5,256,64]{1,2,0:T(8,128)(2,1)S(1)}, bf16[5,256,64]{2,1,0:T(8,128)(2,1)S(1)}, bf16[5,256,64]{2,1,0:T(8,128)(2,1)S(1)}, bf16[5,256,64]{2,1,0:T(8,128)(2,1)S(1)}, /*index=5*/s32[]{:T(128)}) while((s32[]{:T(128)}, bf16[5,256,64]{1,2,0:T(8,128)(2,1)S(1)}, bf16[5,256,64]{2,1,0:T(8,128)(2,1)S(1)}, ...), condition=%wide.region_10.10_spmd, body=%wide.region_7.9_spmd.sunk | while | flops 17251840 | bytes 1023045 | solution.py:102
  67.2 0.7 copy-done.8
  68.1 0.5 convolution_convert_fusion.7
  69.2 2.6 %while.26 = (s32[]{:T(128)}, bf16[5,256,64]{1,2,0:T(8,128)(2,1)S(1)}, bf16[5,256,64]{2,1,0:T(8,128)(2,1)S(1)}, bf16[5,256,64]{2,1,0:T(8,128)(2,1)S(1)}, bf16[5,256,64]{2,1,0:T(8,128)(2,1)S(1)}, /*index=5*/s32[]{:T(128)}) while((s32[]{:T(128)}, bf16[5,256,64]{1,2,0:T(8,128)(2,1)S(1)}, bf16[5,256,64]{2,1,0:T(8,128)(2,1)S(1)}, ...), condition=%wide.region_10.10_spmd, body=%wide.region_7.9_spmd.sunk | while | flops 17251840 | bytes 1023045 | solution.py:102
  72.2 0.7 copy-done.8
  (87 shorter events, 9.8 us)
Async XLA Ops:
  0.0 54.9 %copy-start = (bf16[320,320]{1,0:T(8,128)(2,1)S(1)}, bf16[320,320]{1,0:T(8,128)(2,1)}, u32[]{:S(2)}) copy-start(bf16[320,320]{1,0:T(8,128)(2,1)} %param.16) | copy-start | bytes 614404
  0.0 28.1 %copy-start.5 = (bf16[320,960]{1,0:T(8,128)(2,1)S(1)}, bf16[320,960]{1,0:T(8,128)(2,1)}, u32[]{:S(2)}) copy-start(bf16[320,960]{1,0:T(8,128)(2,1)} %param.15) | copy-start | bytes 1843204
  4.5 27.5 %collective-permute-start = (bf16[4,64,320]{2,1,0:T(8,128)(2,1)}, bf16[4,64,320]{2,1,0:T(8,128)(2,1)S(1)}, u32[]{:S(2)}, u32[]{:S(2)}) collective-permute-start(bf16[4,64,320]{2,1,0:T(8,128)(2,1)} %get-tuple-element.125), channel_id=1, source_target_pairs={{0,4},{4,8},{8,12},{1,5},{5,9},{9,13},{2,6},{6,10},{10,14},{3,7},{... | collective-permute-start | bytes 491528 | tf_op jit(solution)/shard_map/ppermute | solution.py:40
  9.5 22.6 %collective-permute-start.1 = (bf16[4,64,320]{2,1,0:T(8,128)(2,1)}, bf16[4,64,320]{2,1,0:T(8,128)(2,1)}, u32[]{:S(2)}, u32[]{:S(2)}) collective-permute-start(bf16[4,64,320]{2,1,0:T(8,128)(2,1)} %get-tuple-element.126), channel_id=1, source_target_pairs={{4,0},{8,4},{12,8},{5,1},{9,5},{13,9},{6,2},{10,6},{14,10},{7,3},{... | collective-permute-start | bytes 491528 | tf_op jit(solution)/shard_map/ppermute | solution.py:43
  29.0 2.0 %copy-start.2 = (bf16[8,64,320]{2,1,0:T(8,128)(2,1)S(1)}, bf16[8,64,320]{2,1,0:T(8,128)(2,1)}, u32[]{:S(2)}) copy-start(bf16[8,64,320]{2,1,0:T(8,128)(2,1)} %param.12) | copy-start | bytes 983044
  53.9 1.1 %copy-start.4 = (f32[512,320]{0,1:T(8,128)S(1)}, f32[512,320]{0,1:T(8,128)}, u32[]{:S(2)}) copy-start(f32[512,320]{0,1:T(8,128)} %copy.31) | copy-start | bytes 1966084
  55.6 7.3 %copy-start.1 = (bf16[320,960]{1,0:T(8,128)(2,1)S(1)}, bf16[320,960]{1,0:T(8,128)(2,1)}, u32[]{:S(2)}) copy-start(bf16[320,960]{1,0:T(8,128)(2,1)} %param.18) | copy-start | bytes 1843204
  55.6 7.3 %copy-start.3 = (bf16[320,320]{1,0:T(8,128)(2,1)S(1)}, bf16[320,320]{1,0:T(8,128)(2,1)}, u32[]{:S(2)}) copy-start(bf16[320,320]{1,0:T(8,128)(2,1)} %param.19) | copy-start | bytes 614404
  55.6 7.3 %copy-start.6 = (f32[320]{0:T(512)S(1)}, f32[320]{0:T(512)}, u32[]{:S(2)}) copy-start(f32[320]{0:T(512)} %param.17) | copy-start | bytes 3844
  55.7 4.5 %collective-permute-start.2 = (bf16[1,2,64,320]{3,2,1,0:T(8,128)(2,1)S(1)}, bf16[1,2,64,320]{3,2,1,0:T(8,128)(2,1)S(1)}, u32[]{:S(2)}, u32[]{:S(2)}) collective-permute-start(bf16[1,2,64,320]{3,2,1,0:T(8,128)(2,1)S(1)} %get-tuple-element.124), channel_id=1, source_target_pairs={{0,1},{1,2},{2,3},{3,0},{4,5},{5,6},{6,7},{7,4},{8,9},{9,10},{10,1... | collective-permute-start | bytes 245768 | tf_op jit(solution)/shard_map/ppermute | solution.py:30
  55.7 5.7 %collective-permute-start.3 = (bf16[1,2,64,320]{3,2,1,0:T(8,128)(2,1)S(1)}, bf16[1,2,64,320]{3,2,1,0:T(8,128)(2,1)S(1)}, u32[]{:S(2)}, u32[]{:S(2)}) collective-permute-start(bf16[1,2,64,320]{3,2,1,0:T(8,128)(2,1)S(1)} %get-tuple-element.123), channel_id=1, source_target_pairs={{0,2},{1,3},{2,0},{3,1},{4,6},{5,7},{6,4},{7,5},{8,10},{9,11},{10,... | collective-permute-start | bytes 245768 | tf_op jit(solution)/shard_map/ppermute | solution.py:30
  57.3 4.6 %collective-permute-start.4 = (bf16[1,2,64,320]{3,2,1,0:T(8,128)(2,1)S(1)}, bf16[1,2,64,320]{3,2,1,0:T(8,128)(2,1)S(1)}, u32[]{:S(2)}, u32[]{:S(2)}) collective-permute-start(bf16[1,2,64,320]{3,2,1,0:T(8,128)(2,1)S(1)} %get-tuple-element.122), channel_id=1, source_target_pairs={{0,3},{1,0},{2,1},{3,2},{4,7},{5,4},{6,5},{7,6},{8,11},{9,8},{10,9... | collective-permute-start | bytes 245768 | tf_op jit(solution)/shard_map/ppermute | solution.py:30
  64.2 2.7 %copy-start.7 = (bf16[2,256,320]{1,2,0:T(8,128)(2,1)S(1)}, bf16[2,256,320]{1,2,0:T(8,128)(2,1)}, u32[]{:S(2)}) copy-start(bf16[2,256,320]{1,2,0:T(8,128)(2,1)} %get-tuple-element.248) | copy-start | bytes 983044 | tf_op jit(solution)/shard_map/while
  67.2 0.7 copy-start.8
  69.2 2.7 %copy-start.7 = (bf16[2,256,320]{1,2,0:T(8,128)(2,1)S(1)}, bf16[2,256,320]{1,2,0:T(8,128)(2,1)}, u32[]{:S(2)}) copy-start(bf16[2,256,320]{1,2,0:T(8,128)(2,1)} %get-tuple-element.248) | copy-start | bytes 983044 | tf_op jit(solution)/shard_map/while
  72.2 0.7 copy-start.8
